TPU v7x, 256 devices: a whole 4x4x8 slice. The times are simulated.
256 devices in a mesh: rows: 32 (over y, z), mem: 8 (over x, core).
Axes of the slice: x: 4, y: 4, z: 8, core: 2. Of those that a mesh axis runs over, the one named last changes fastest.
Arguments:
- ensemble: float32 [64, 32, 192, 384], P('mem', None, 'rows'), may hold values from 0 to 2
- courant: float32 [3, 32, 192, 384], P(None, None, 'rows'), may hold values from -0.22 to 0.22
- obs_column: int32 [512], P('rows'), may hold values from 0 to 73727, as said below
- obs_value: float32 [32, 512], P(None, 'rows'), may hold values from -6 to 6
- obs_var: float32 [32, 512], P(None, 'rows'), may hold values from 0.5 to 8
Outputs:
- analysis: float32 [64, 32, 192, 384], P('mem', None, 'rows')
Inputs may be any that keep to these rules, and one draw needn't show every extreme that they name: `obs_column`: entry p is x * 384 + y with x from (p // 16) * 6 to (p // 16) * 6 + 5.
All inputs are finite; a program needn't handle non-finite values.
Results may differ from a plain program's by a relative error of at most 0.0003.
Values sent between devices are 32-bit elements; how exact they have to be, the bound alone decides.
No kernel may reach another device: no remote copies, remote signals or barrier semaphores. Data moves between devices by JAX's collectives and lax.ppermute only.
A program may use at most 128 MiB of HBM per device.

v0:
```python
import jax
import jax.numpy as jnp
from jax import lax
from jax.sharding import PartitionSpec as P

STEPS = 3
NS_ITERS = 4
DIFFUSION = 0.05


def padded_2(cells, sides, width):
    for axis, dim in sides:
        count = lax.axis_size(axis)
        ends = count - 1
        head = lax.slice_in_dim(cells, 0, width, axis=dim)
        tail = lax.slice_in_dim(cells, cells.shape[dim] - width, cells.shape[dim], axis=dim)
        cells = jnp.concatenate(
            [
                lax.ppermute(tail, axis, [(i, (i + 1) % count) for i in range(ends)]),
                cells,
                lax.ppermute(head, axis, [((i + 1) % count, i) for i in range(ends)]),
            ],
            axis=dim,
        )
    return cells


def joined_along(parts, dim):
    parts = jnp.moveaxis(parts, 0, dim)
    lengths = parts.shape
    return parts.reshape(*lengths[:dim], lengths[dim] * lengths[dim + 1], *lengths[dim + 2 :])


def from_everyone(shard, axis):
    copies = jnp.broadcast_to(shard, (lax.axis_size(axis), *shard.shape))
    return lax.all_to_all(copies, axis, split_axis=0, concat_axis=0, tiled=True)


def collect(shard, axis, dim):
    return joined_along(from_everyone(shard, axis), dim)


def over_copies(shard, axis):
    everything = from_everyone(shard, axis)
    return jnp.sum(everything, axis=0)


def packed_total(arrays, axis):
    ends = [0]
    for a in arrays:
        ends.append(ends[-1] + a.size)
    so_far = over_copies(jnp.concatenate([a.ravel() for a in arrays]), axis)
    return tuple((so_far[b:e].reshape(a.shape) for a, b, e in zip(arrays, ends, ends[1:])))


def advance(padded, courant):
    center = padded[:, :, 1:-1, :]
    below_x = padded[:, :, :-2, :]
    above_x = padded[:, :, 2:, :]
    padded_y = jnp.pad(center, ((0, 0), (0, 0), (0, 0), (1, 1)))
    below_y = padded_y[:, :, :, :-2]
    above_y = padded_y[:, :, :, 2:]
    padded_z = jnp.pad(center, ((0, 0), (1, 1), (0, 0), (0, 0)))
    below_z = padded_z[:, :-2]
    above_z = padded_z[:, 2:]
    change = jnp.zeros_like(center)
    for component, below, above in (
        (0, below_x, above_x),
        (1, below_y, above_y),
        (2, below_z, above_z),
    ):
        velocity = courant[component][None]
        change = (
            change
            - jnp.maximum(velocity, 0.0) * (center - below)
            - jnp.minimum(velocity, 0.0) * (above - center)
            + DIFFUSION * (above + below - 2.0 * center)
        )
    return center + change


def gram_terms(profiles, obs_value, obs_var):
    members_all = profiles.shape[0]
    center = jnp.mean(profiles, axis=0)
    scaling = 1.0 / jnp.sqrt((members_all - 1.0) * obs_var)
    scaled = ((profiles - center[None]) * scaling[None]).reshape(members_all, -1)
    innovation = ((obs_value - center) / jnp.sqrt(obs_var)).reshape(-1)
    gram_part = jnp.dot(scaled, scaled.T, precision=lax.Precision.HIGHEST)
    pull_part = jnp.dot(scaled, innovation, precision=lax.Precision.HIGHEST)
    return (gram_part, pull_part)


def mixing(gram_sum, pull_sum):
    members_all = gram_sum.shape[0]
    identity_matrix = jnp.eye(members_all, dtype=jnp.float32)
    system = identity_matrix + gram_sum
    frobenius = jnp.sqrt(jnp.sum(system * system))

    def newton(iteration, carry):
        iterate, inverse_root = carry
        factor = 0.5 * (
            3.0 * identity_matrix - jnp.dot(inverse_root, iterate, precision=lax.Precision.HIGHEST)
        )
        return (
            jnp.dot(iterate, factor, precision=lax.Precision.HIGHEST),
            jnp.dot(factor, inverse_root, precision=lax.Precision.HIGHEST),
        )

    iterate, inverse_root = lax.fori_loop(
        0, NS_ITERS, newton, (system / frobenius, identity_matrix)
    )
    root_inverse = inverse_root / jnp.sqrt(frobenius)
    mean_shift = jnp.dot(
        root_inverse,
        jnp.dot(root_inverse, pull_sum, precision=lax.Precision.HIGHEST),
        precision=lax.Precision.HIGHEST,
    ) / jnp.sqrt(members_all - 1.0)
    centering = identity_matrix - 1.0 / members_all
    return 1.0 / members_all + jnp.dot(
        centering, mean_shift[:, None] + root_inverse, precision=lax.Precision.HIGHEST
    )


def per_device(ensemble, courant, obs_column, obs_value, obs_var):
    rows_local = ensemble.shape[2]
    width_y = ensemble.shape[3]
    position = lax.axis_index("rows")
    concentration = ensemble
    for step_index in range(STEPS):
        padded = padded_2(concentration, (("rows", 2),), 1)
        concentration = advance(padded, courant)
    members_dev = concentration.shape[0]
    state_vectors = concentration.reshape(members_dev, concentration.shape[1], rows_local * width_y)
    local_column = obs_column - position * (rows_local * width_y)
    profiles = jnp.take(state_vectors, local_column, axis=2)
    gathered = collect(profiles, "mem", 0)
    gram_part, pull_part = gram_terms(gathered, obs_value, obs_var)
    gram_sum, pull_sum = packed_total((gram_part, pull_part), "rows")
    transform_weights = mixing(gram_sum, pull_sum)
    first_member = lax.axis_index("mem") * members_dev
    own_columns = lax.dynamic_slice_in_dim(transform_weights, first_member, members_dev, 1)
    updated_ensemble = jnp.einsum(
        "jk,jzc->kzc",
        own_columns,
        lax.all_gather(state_vectors, "mem", axis=0, tiled=True),
        precision=lax.Precision.HIGHEST,
    )
    return updated_ensemble.reshape(concentration.shape)


def solution(mesh):
    return jax.shard_map(
        per_device,
        mesh=mesh,
        in_specs=(
            P("mem", None, "rows", None),
            P(None, None, "rows", None),
            P("rows"),
            P(None, "rows"),
            P(None, "rows"),
        ),
        out_specs=P("mem", None, "rows", None),
        check_vma=False,
    )
```

profile of v0, /device:TPU:1, one launch (start us, length us, event | category | flops | bytes accessed | tf_op | source)
XLA Modules:
  0.0 191.4 jit_solution(7177170914299280212)
XLA Ops:
  6.5 0.0 all-gather.2.cloned.1.call-start
  6.5 1.3 fusion.77
  7.9 4.4 %collective-permute-start = (f32[8,32,1,384]{3,1,2,0:T(8,128)S(1)}, f32[8,32,1,384]{3,1,2,0:T(8,128)S(1)}, u32[]{:S(2)}, u32[]{:S(2)}) collective-permute-start(f32[8,32,1,384]{3,1,2,0:T(8,128)S(1)} %get-tuple-element.60), channel_id=1, source_target_pairs={{0,8},{8,16},{16,24},{24,32},{32,40},{40,48},{48,56},{56,64},{64,7... | collective-permute-start | bytes 1179656 | tf_op jit(solution)/shard_map/ppermute | solution.py:19
  12.3 1.3 collective-permute-start.1
  13.6 1.3 maximum_bitcast_fusion.2
  14.9 5.1 %collective-permute-done = f32[8,32,1,384]{3,1,2,0:T(8,128)S(1)} collective-permute-done((f32[8,32,1,384]{3,1,2,0:T(8,128)S(1)}, f32[8,32,1,384]{3,1,2,0:T(8,128)S(1)}, u32[]{:S(2)}, u32[]{:S(2)}) %collective-permute-start) | collective-permute-done | bytes 393248 | tf_op jit(solution)/shard_map/ppermute | solution.py:19
  20.0 4.2 %collective-permute-done.1 = f32[8,32,1,384]{3,1,2,0:T(8,128)S(1)} collective-permute-done((f32[8,32,1,384]{3,1,2,0:T(8,128)S(1)}, f32[8,32,1,384]{3,1,2,0:T(8,128)S(1)}, u32[]{:S(2)}, u32[]{:S(2)}) %collective-permute-start.1) | collective-permute-done | bytes 393248 | tf_op jit(solution)/shard_map/ppermute | solution.py:21
  24.2 0.0 copy-done.1
  24.2 3.7 %fusion.48 = f32[8,32,6,384]{3,1,2,0:T(8,128)S(1)} fusion(f32[8,32,6,384]{3,1,2,0:T(8,128)S(1)} %copy-done.1, f32[8,32,1,384]{3,1,2,0:T(8,128)S(1)} %collective-permute-done.1, f32[8,32,1,384]{3,1,2,0:T(8,128)S(1)} %collective-permute-done, f32[32,6,384]{2,0,1:T(8,128)S(1)} %get-tuple-element.65, f32[32,6,384]{2,0,1:T(8,128)S(1)} %get-tuple-element.66, ...), kind=kLoop, calls=%fused_computation.68 | loop fusion | flops 20054016 | bytes 7274496 | tf_op jit(solution)/shard_map/add | solution.py:79
  27.9 0.1 fusion.76
  28.0 3.6 %collective-permute-start.2 = (f32[8,32,1,384]{3,1,2,0:T(8,128)S(1)}, f32[8,32,1,384]{3,1,2,0:T(8,128)S(1)}, u32[]{:S(2)}, u32[]{:S(2)}) collective-permute-start(f32[8,32,1,384]{3,1,2,0:T(8,128)S(1)} %get-tuple-element.58), channel_id=1, source_target_pairs={{0,8},{8,16},{16,24},{24,32},{32,40},{40,48},{48,56},{56,64},{64,7... | collective-permute-start | bytes 1179656 | tf_op jit(solution)/shard_map/ppermute | solution.py:19
  31.6 1.3 collective-permute-start.3
  32.9 5.5 %collective-permute-done.2 = f32[8,32,1,384]{3,1,2,0:T(8,128)S(1)} collective-permute-done((f32[8,32,1,384]{3,1,2,0:T(8,128)S(1)}, f32[8,32,1,384]{3,1,2,0:T(8,128)S(1)}, u32[]{:S(2)}, u32[]{:S(2)}) %collective-permute-start.2) | collective-permute-done | bytes 393248 | tf_op jit(solution)/shard_map/ppermute | solution.py:19
  38.4 5.7 %collective-permute-done.3 = f32[8,32,1,384]{3,1,2,0:T(8,128)S(1)} collective-permute-done((f32[8,32,1,384]{3,1,2,0:T(8,128)S(1)}, f32[8,32,1,384]{3,1,2,0:T(8,128)S(1)}, u32[]{:S(2)}, u32[]{:S(2)}) %collective-permute-start.3) | collective-permute-done | bytes 393248 | tf_op jit(solution)/shard_map/ppermute | solution.py:21
  44.1 3.7 %fusion.31 = f32[8,32,6,384]{3,1,2,0:T(8,128)S(1)} fusion(f32[8,32,6,384]{3,1,2,0:T(8,128)S(1)} %fusion.48, f32[8,32,1,384]{3,1,2,0:T(8,128)S(1)} %collective-permute-done.3, f32[8,32,1,384]{3,1,2,0:T(8,128)S(1)} %collective-permute-done.2, f32[32,6,384]{2,0,1:T(8,128)S(1)} %get-tuple-element.65, f32[32,6,384]{2,0,1:T(8,128)S(1)} %get-tuple-element.66, ...), kind=kLoop, calls=%fused_computation.49 | loop fusion | flops 20054016 | bytes 7274496 | tf_op jit(solution)/shard_map/add | solution.py:79
  47.8 0.1 fusion.75
  47.9 4.0 %collective-permute-start.4 = (f32[8,32,1,384]{3,1,2,0:T(8,128)S(1)}, f32[8,32,1,384]{3,1,2,0:T(8,128)S(1)}, u32[]{:S(2)}, u32[]{:S(2)}) collective-permute-start(f32[8,32,1,384]{3,1,2,0:T(8,128)S(1)} %get-tuple-element.56), channel_id=1, source_target_pairs={{0,8},{8,16},{16,24},{24,32},{32,40},{40,48},{48,56},{56,64},{64,7... | collective-permute-start | bytes 1179656 | tf_op jit(solution)/shard_map/ppermute | solution.py:19
  51.9 1.3 collective-permute-start.5
  53.2 4.5 %collective-permute-done.4 = f32[8,32,1,384]{3,1,2,0:T(8,128)S(1)} collective-permute-done((f32[8,32,1,384]{3,1,2,0:T(8,128)S(1)}, f32[8,32,1,384]{3,1,2,0:T(8,128)S(1)}, u32[]{:S(2)}, u32[]{:S(2)}) %collective-permute-start.4) | collective-permute-done | bytes 393248 | tf_op jit(solution)/shard_map/ppermute | solution.py:19
  57.7 3.9 %collective-permute-done.5 = f32[8,32,1,384]{3,1,2,0:T(8,128)S(1)} collective-permute-done((f32[8,32,1,384]{3,1,2,0:T(8,128)S(1)}, f32[8,32,1,384]{3,1,2,0:T(8,128)S(1)}, u32[]{:S(2)}, u32[]{:S(2)}) %collective-permute-start.5) | collective-permute-done | bytes 393248 | tf_op jit(solution)/shard_map/ppermute | solution.py:21
  61.5 3.7 %fusion.14 = f32[8,32,6,384]{3,1,2,0:T(8,128)S(1)} fusion(f32[8,32,6,384]{3,1,2,0:T(8,128)S(1)} %fusion.31, f32[8,32,1,384]{3,1,2,0:T(8,128)S(1)} %collective-permute-done.5, f32[8,32,1,384]{3,1,2,0:T(8,128)S(1)} %collective-permute-done.4, f32[32,6,384]{2,0,1:T(8,128)S(1)} %get-tuple-element.65, f32[32,6,384]{2,0,1:T(8,128)S(1)} %get-tuple-element.66, ...), kind=kLoop, calls=%fused_computation.30 | loop fusion | flops 20054016 | bytes 7274496 | tf_op jit(solution)/shard_map/add | solution.py:79
  65.3 2.8 %copy.24 = f32[8,32,6,384]{3,0,2,1:T(8,128)} copy(f32[8,32,6,384]{3,1,2,0:T(8,128)S(1)} %fusion.14) | data formatting | bytes 4718592 | tf_op jit(solution)/shard_map/add | solution.py:79
  68.1 0.0 all-gather.2.cloned.1.call-update
  68.1 0.6 copy-done.4
  68.7 1.0 copy-done
  69.7 5.9 %copy.25 = f32[8,32,2304]{1,0,2:T(8,128)} copy(f32[8,32,2304]{2,0,1:T(8,128)S(1)} %bitcast.72) | data formatting | bytes 4718592 | tf_op jit(solution)/shard_map/reshape | solution.py:133
  75.6 4.3 %gather_fusion = f32[16,8,32]{2,1,0:T(8,128)S(1)} fusion(f32[8,32,2304]{1,0,2:T(8,128)} %copy.25, s32[1024]{0:T(1024)S(1)} %pad_clamp_fusion), kind=kCustom, calls=%fused_computation | custom fusion | bytes 32832 | tf_op jit(solution)/shard_map/jit(_take)/gather | solution.py:135
  79.9 0.1 select_bitcast_fusion
  80.1 0.3 reshape.69
  80.3 14.6 %all_to_all.11 = f32[8,1,4096]{2,1,0:T(1,128)S(1)} all-to-all(f32[8,1,4096]{2,1,0:T(1,128)S(1)} %reshape.69), channel_id=1, replica_groups=mesh['rows'=32,'mem'=8] {'mem'}, dimensions={0} | all-to-all | bytes 262144 | tf_op jit(solution)/shard_map/all_to_all | solution.py:36
  95.0 0.6 broadcast.111
  95.6 1.0 reduce.3
  96.5 0.2 reshape.70
  96.7 0.1 bitcast_reduce_fusion
  96.9 0.7 convolution_bitcast_fusion.1
  97.6 0.1 reshape.47
  97.8 0.6 convolution_bitcast_fusion.4
  98.4 1.1 broadcast_in_dim.25
  99.5 10.2 %all-to-all-start.1 = ((f32[32,1,4160]{2,1,0:T(1,128)}), f32[32,1,4160]{2,1,0:T(1,128)S(1)}, u32[]{:S(2)}, u32[]{:S(2)}) async-start(f32[32,1,4160]{2,1,0:T(1,128)} %broadcast_in_dim.25), calls=%async_computation.1 | async-start | bytes 1081344 | tf_op jit(solution)/shard_map/all_to_all | solution.py:36
  109.7 0.1 reshape.51
  109.8 14.8 %all-to-all-done.1 = f32[32,1,4160]{2,1,0:T(1,128)S(1)} async-done(((f32[32,1,4160]{2,1,0:T(1,128)}), f32[32,1,4160]{2,1,0:T(1,128)S(1)}, u32[]{:S(2)}, u32[]{:S(2)}) %all-to-all-start.1) | async-done | bytes 532512 | tf_op jit(solution)/shard_map/all_to_all | solution.py:36
  124.6 0.3 reduce_sum.28
  124.9 0.7 multiply_reduce_fusion
  125.6 0.1 reshape.49
  126.4 0.1 copy.30
  126.5 2.6 %while.13 = (s32[]{:T(128)}, f32[64,64]{0,1:T(8,128)S(1)}, f32[64,64]{1,0:T(8,128)S(1)}, s32[]{:T(128)}) while((s32[]{:T(128)}, f32[64,64]{0,1:T(8,128)S(1)}, f32[64,64]{1,0:T(8,128)S(1)}, s32[]{:T(128)}) %tuple.37), condition=%wide.region_4.5_spmd.clone, body=%wide.region_3.4_spmd.clone.sunk | while | flops 9453570 | bytes 213045 | solution.py:109
  126.5 0.2 fusion.102
  126.7 0.2 fusion.103
  126.9 0.2 convolution_bitcast_fusion.6
  127.1 0.2 fusion.102
  127.3 0.2 fusion.103
  127.5 0.2 convolution_bitcast_fusion.6
  127.8 0.2 fusion.102
  128.0 0.2 fusion.103
  128.2 0.2 convolution_bitcast_fusion.6
  128.4 0.2 fusion.102
  128.6 0.2 fusion.103
  128.8 0.2 convolution_bitcast_fusion.6
  129.1 0.2 convolution_bitcast_fusion.3
  129.2 0.2 fusion.57
  129.4 0.3 fusion.61
  129.7 40.7 %all-gather.2.cloned.1.call-done = f32[64,32,2304]{2,0,1:T(8,128)} async-done(((f32[8,32,2304]{2,0,1:T(8,128)}), f32[64,32,2304]{2,0,1:T(8,128)}) %all-gather.2.cloned.1.call-update) | async-done | bytes 18874384 | tf_op jit(solution)/shard_map/all_gather | solution.py:145
  170.4 12.0 %fusion.69 = f32[8,32,2304]{2,0,1:T(8,128)S(1)} fusion(f32[64,32,2304]{2,0,1:T(8,128)} %all-gather.2.cloned.1.call-done, f32[64,64]{0,1:T(8,128)S(1)} %fusion.61, s32[]{:T(128)S(6)} %select_n.14), kind=kOutput, calls=%fused_computation.113 | convolution fusion | flops 452985344 | bytes 21237764 | tf_op jit(solution)/shard_map/jk,jzc->kzc/dot_general | solution.py:142
  182.4 2.1 %copy.31 = f32[8,32,6,384]{3,1,2,0:T(8,128)} copy(f32[8,32,6,384]{3,0,2,1:T(8,128)S(1)} %bitcast.73) | data formatting | bytes 4718592 | tf_op jit(solution)/shard_map/reshape | solution.py:148
  (25 shorter events, 0.2 us)
Async XLA Ops:
  6.5 17.7 %copy-start.1 = (f32[8,32,6,384]{3,1,2,0:T(8,128)S(1)}, f32[8,32,6,384]{3,1,2,0:T(8,128)}, u32[]{:S(2)}) copy-start(f32[8,32,6,384]{3,1,2,0:T(8,128)} %param.7) | copy-start | bytes 7077892
  6.5 163.9 %all-gather.2.cloned.1.call-start = ((), (), s32[]{:S(2)}) async-start(), calls=%async_computation.2 | async-start | bytes 21233664 | tf_op jit(solution)/shard_map/all_gather | solution.py:145
  7.9 12.1 %collective-permute-start = (f32[8,32,1,384]{3,1,2,0:T(8,128)S(1)}, f32[8,32,1,384]{3,1,2,0:T(8,128)S(1)}, u32[]{:S(2)}, u32[]{:S(2)}) collective-permute-start(f32[8,32,1,384]{3,1,2,0:T(8,128)S(1)} %get-tuple-element.60), channel_id=1, source_target_pairs={{0,8},{8,16},{16,24},{24,32},{32,40},{40,48},{48,56},{56,64},{64,7... | collective-permute-start | bytes 1179656 | tf_op jit(solution)/shard_map/ppermute | solution.py:19
  12.3 11.9 %collective-permute-start.1 = (f32[8,32,1,384]{3,1,2,0:T(8,128)S(1)}, f32[8,32,1,384]{3,1,2,0:T(8,128)S(1)}, u32[]{:S(2)}, u32[]{:S(2)}) collective-permute-start(f32[8,32,1,384]{3,1,2,0:T(8,128)S(1)} %get-tuple-element.61), channel_id=1, source_target_pairs={{8,0},{16,8},{24,16},{32,24},{40,32},{48,40},{56,48},{64,56},{72,6... | collective-permute-start | bytes 1179656 | tf_op jit(solution)/shard_map/ppermute | solution.py:21
  28.0 10.4 %collective-permute-start.2 = (f32[8,32,1,384]{3,1,2,0:T(8,128)S(1)}, f32[8,32,1,384]{3,1,2,0:T(8,128)S(1)}, u32[]{:S(2)}, u32[]{:S(2)}) collective-permute-start(f32[8,32,1,384]{3,1,2,0:T(8,128)S(1)} %get-tuple-element.58), channel_id=1, source_target_pairs={{0,8},{8,16},{16,24},{24,32},{32,40},{40,48},{48,56},{56,64},{64,7... | collective-permute-start | bytes 1179656 | tf_op jit(solution)/shard_map/ppermute | solution.py:19
  31.6 12.5 %collective-permute-start.3 = (f32[8,32,1,384]{3,1,2,0:T(8,128)S(1)}, f32[8,32,1,384]{3,1,2,0:T(8,128)S(1)}, u32[]{:S(2)}, u32[]{:S(2)}) collective-permute-start(f32[8,32,1,384]{3,1,2,0:T(8,128)S(1)} %get-tuple-element.59), channel_id=1, source_target_pairs={{8,0},{16,8},{24,16},{32,24},{40,32},{48,40},{56,48},{64,56},{72,6... | collective-permute-start | bytes 1179656 | tf_op jit(solution)/shard_map/ppermute | solution.py:21
  47.9 9.8 %collective-permute-start.4 = (f32[8,32,1,384]{3,1,2,0:T(8,128)S(1)}, f32[8,32,1,384]{3,1,2,0:T(8,128)S(1)}, u32[]{:S(2)}, u32[]{:S(2)}) collective-permute-start(f32[8,32,1,384]{3,1,2,0:T(8,128)S(1)} %get-tuple-element.56), channel_id=1, source_target_pairs={{0,8},{8,16},{16,24},{24,32},{32,40},{40,48},{48,56},{56,64},{64,7... | collective-permute-start | bytes 1179656 | tf_op jit(solution)/shard_map/ppermute | solution.py:19
  51.9 9.6 %collective-permute-start.5 = (f32[8,32,1,384]{3,1,2,0:T(8,128)S(1)}, f32[8,32,1,384]{3,1,2,0:T(8,128)S(1)}, u32[]{:S(2)}, u32[]{:S(2)}) collective-permute-start(f32[8,32,1,384]{3,1,2,0:T(8,128)S(1)} %get-tuple-element.57), channel_id=1, source_target_pairs={{8,0},{16,8},{24,16},{32,24},{40,32},{48,40},{56,48},{64,56},{72,6... | collective-permute-start | bytes 1179656 | tf_op jit(solution)/shard_map/ppermute | solution.py:21
  68.1 0.7 copy-start.4
  68.1 1.7 copy-start
  75.6 21.2 %copy-start.2 = (f32[32,16]{0,1:T(8,128)S(1)}, f32[32,16]{0,1:T(8,128)}, u32[]{:S(2)}) copy-start(f32[32,16]{0,1:T(8,128)} %param.11) | copy-start | bytes 6148
  75.6 21.2 %copy-start.3 = (f32[32,16]{0,1:T(8,128)S(1)}, f32[32,16]{0,1:T(8,128)}, u32[]{:S(2)}) copy-start(f32[32,16]{0,1:T(8,128)} %param.10) | copy-start | bytes 6148
  99.5 25.1 %all-to-all-start.1 = ((f32[32,1,4160]{2,1,0:T(1,128)}), f32[32,1,4160]{2,1,0:T(1,128)S(1)}, u32[]{:S(2)}, u32[]{:S(2)}) async-start(f32[32,1,4160]{2,1,0:T(1,128)} %broadcast_in_dim.25), calls=%async_computation.1 | async-start | bytes 1081344 | tf_op jit(solution)/shard_map/all_to_all | solution.py:36
Sparse Core Ops, SparseCore 0:
  68.2 102.1 all-gather.1
where the time goes:
time: 192 us; the launch traced here: 191 us
  waiting for transfers between devices  84.3 us (44%)
  starting transfers between devices  26.1 us (14%)
  local copies, waits for them, and re-layouts  20.6 us (11%)
  matrix products  16.3 us (8%)
  other arithmetic  14.8 us (8%)
  blocking collectives  14.6 us (8%)
  between operations  14.4 us (8%)
    all_gather x1, waiting for transfers between devices, per_device(): lax.all_gather(state_vectors, 'mem', axis=0, tiled=True)  40.7 us
    ppermute x3, waiting for transfers between devices, padded_2(): lax.ppermute(tail, axis, [(i, (i + 1) % count) for i in range(ends)])  15.1 us
    all_to_all x1, waiting for transfers between devices, from_everyone(): return lax.all_to_all(copies, axis, split_axis=0, concat_axis=0, tiled=True)  14.8 us
    all_to_all x1, blocking collectives, from_everyone(): return lax.all_to_all(copies, axis, split_axis=0, concat_axis=0, tiled=True)  14.6 us
    ppermute x3, waiting for transfers between devices, padded_2(): lax.ppermute(head, axis, [((i + 1) % count, i) for i in range(ends)])  13.7 us
    ppermute x3, starting transfers between devices, padded_2(): lax.ppermute(tail, axis, [(i, (i + 1) % count) for i in range(ends)])  12 us
    dot_general x1, matrix products, per_device(): jnp.einsum('jk,jzc->kzc', own_columns, lax.all_gather(state_vectors, 'mem...  12 us
    add x3, other arithmetic, advance(): return center + change  11.2 us
  transfers between devices with their start and end apart: 8, of which 8 were waited for; matrix products, arithmetic and copies ran while one was open for 11% of the time, Pallas kernels for 0%

commit v1 on v0

--- a/solution.py
+++ b/solution.py
@@ -6,6 +6,38 @@
 STEPS = 3
 NS_ITERS = 4
 DIFFUSION = 0.05
+
+
+def part_the_sums_all(m, row_dim):
+    m = jnp.moveaxis(m, 0, row_dim)
+    local_part = m.shape
+    return m.reshape(
+        *local_part[:row_dim],
+        local_part[row_dim] * local_part[row_dim + 1],
+        *local_part[row_dim + 2 :]
+    )
+
+
+def floor_carry(array_here, ax_name, at_axis):
+    extent = lax.psum(1, axis_name=ax_name)
+    history = []
+    for pp in tuple(range(extent)):
+        history.append((pp, (pp + 1) % extent))
+    queue = []
+    for w, k in history:
+        queue.append((k, w))
+    passed, state_now = ([], [])
+    for k0 in tuple(range(extent - 1)):
+        if k0 % 2 == 0:
+            passed.append(lax.ppermute(passed[-1] if passed else array_here, ax_name, perm=history))
+        else:
+            state_now.append(
+                lax.ppermute(state_now[-1] if state_now else array_here, ax_name, queue)
+            )
+    main = jnp.stack([*passed[::-1], array_here, *state_now], axis=0)
+    formed = lax.axis_index(ax_name) - len(passed)
+    main = main[(jnp.arange(extent) - formed) % extent]
+    return part_the_sums_all(main, at_axis)
 
 
 def padded_2(cells, sides, width):
@@ -142,7 +174,7 @@
     updated_ensemble = jnp.einsum(
         "jk,jzc->kzc",
         own_columns,
-        lax.all_gather(state_vectors, "mem", axis=0, tiled=True),
+        floor_carry(state_vectors, ax_name="mem", at_axis=0),
         precision=lax.Precision.HIGHEST,
     )
     return updated_ensemble.reshape(concentration.shape)

time: 192 us -> 262 us (1.36); the launches traced: 191 us -> 257 us
  local copies, waits for them, and re-layouts: 20.6 us -> 73.5 us
  starting transfers between devices: 26.1 us -> 54.2 us
  blocking collectives: 14.6 us -> 0 us
  between operations: 14.4 us -> 1.18 us
  other arithmetic: 14.8 us -> 22.8 us
  waiting for transfers between devices: 84.3 us -> 91.3 us
    ppermute x0 -> x7, waiting for transfers between devices: none -> 54.7 us  [the longest x3 28.9 us: floor_carry(): lax.ppermute(state_now[-1] if state_now else array_here, ax_name, queue)]
    all_gather x1 -> x0, waiting for transfers between devices: 40.7 us -> none  [per_device(): lax.all_gather(state_vectors, 'mem', axis=0, tiled=True)]
    unnamed x14 -> x39, local copies, waits for them, and re-layouts: 2.17 us -> 23.3 us
    gather x0 -> x1, local copies, waits for them, and re-layouts: none -> 15.3 us  [floor_carry(): main = main[(jnp.arange(extent) - formed) % extent]]
    all_to_all x1 -> x0, blocking collectives: 14.6 us -> none  [from_everyone(): return lax.all_to_all(copies, axis, split_axis=0, concat_axis=0, tiled=True)]
    ppermute x0 -> x7, starting transfers between devices: none -> 13 us  [the longest x4 7.79 us: floor_carry(): lax.ppermute(passed[-1] if passed else array_here, ax_name, perm=history)]
    ppermute x3, waiting for transfers between devices: 15.1 us -> 2.7 us  [padded_2(): lax.ppermute(tail, axis, [(i, (i + 1) % count) for i in range(ends)])]
    all_to_all x1 -> x2, starting transfers between devices: 10.2 us -> 21.2 us  [from_everyone(): return lax.all_to_all(copies, axis, split_axis=0, concat_axis=0, tiled=True)]
  transfers between devices with their start and end apart: 8 -> 15, of which waited for: 8 -> 11; matrix products, arithmetic and copies ran while one was open for 11% -> 22% of each run, Pallas kernels for 0% -> 0%
where the time goes in v1:
time: 262 us; the launch traced here: 257 us
  waiting for transfers between devices  91.3 us (35%)
  local copies, waits for them, and re-layouts  73.5 us (28%)
  starting transfers between devices  54.2 us (21%)
  other arithmetic  22.8 us (9%)
  matrix products  14.1 us (5%)
    ppermute x3, waiting for transfers between devices, floor_carry(): lax.ppermute(state_now[-1] if state_now else array_here, ax_name, queue)  28.9 us
    ppermute x4, waiting for transfers between devices, floor_carry(): lax.ppermute(passed[-1] if passed else array_here, ax_name, perm=history)  25.8 us
    unnamed x39, local copies, waits for them, and re-layouts  23.3 us
    all_to_all x2, starting transfers between devices, from_everyone(): return lax.all_to_all(copies, axis, split_axis=0, concat_axis=0, tiled=True)  21.2 us
    all_to_all x2, waiting for transfers between devices, from_everyone(): return lax.all_to_all(copies, axis, split_axis=0, concat_axis=0, tiled=True)  19.9 us
    ppermute x3, starting transfers between devices, padded_2(): lax.ppermute(tail, axis, [(i, (i + 1) % count) for i in range(ends)])  16.1 us
    gather x1, local copies, waits for them, and re-layouts, floor_carry(): main = main[(jnp.arange(extent) - formed) % extent]  15.3 us
    ppermute x3, waiting for transfers between devices, padded_2(): lax.ppermute(head, axis, [((i + 1) % count, i) for i in range(ends)])  14 us
  transfers between devices with their start and end apart: 15, of which 11 were waited for; matrix products, arithmetic and copies ran while one was open for 22% of the time, Pallas kernels for 0%

profile of v1, /device:TPU:1, one launch (start us, length us, event | category | flops | bytes accessed | tf_op | source)
XLA Modules:
  0.0 257.4 jit_solution(10464091985023362619)
XLA Ops:
  0.0 1.3 fusion.81
  1.3 1.3 collective-permute-start.1
  2.6 5.0 %collective-permute-start = (f32[8,32,1,384]{3,1,2,0:T(8,128)S(1)}, f32[8,32,1,384]{3,1,2,0:T(8,128)S(1)}, u32[]{:S(2)}, u32[]{:S(2)}) collective-permute-start(f32[8,32,1,384]{3,1,2,0:T(8,128)S(1)} %get-tuple-element.60), channel_id=1, source_target_pairs={{0,8},{8,16},{16,24},{24,32},{32,40},{40,48},{48,56},{56,64},{64,7... | collective-permute-start | bytes 1179656 | tf_op jit(solution)/shard_map/ppermute | solution.py:51
  7.6 1.3 maximum_bitcast_fusion.2
  9.0 3.7 %collective-permute-done.1 = f32[8,32,1,384]{3,1,2,0:T(8,128)S(1)} collective-permute-done((f32[8,32,1,384]{3,1,2,0:T(8,128)S(1)}, f32[8,32,1,384]{3,1,2,0:T(8,128)S(1)}, u32[]{:S(2)}, u32[]{:S(2)}) %collective-permute-start.1) | collective-permute-done | bytes 393248 | tf_op jit(solution)/shard_map/ppermute | solution.py:53
  12.7 0.9 collective-permute-done
  13.6 3.7 %fusion.51 = f32[8,32,6,384]{3,1,2,0:T(8,128)S(1)} fusion(f32[8,32,6,384]{3,1,2,0:T(8,128)S(1)} %copy-done.7, f32[8,32,1,384]{3,1,2,0:T(8,128)S(1)} %collective-permute-done.1, f32[8,32,1,384]{3,1,2,0:T(8,128)S(1)} %collective-permute-done, f32[32,6,384]{2,0,1:T(8,128)S(1)} %get-tuple-element.65, f32[32,6,384]{2,0,1:T(8,128)S(1)} %get-tuple-element.66, ...), kind=kLoop, calls=%fused_computation.72 | loop fusion | flops 20054016 | bytes 7274496 | tf_op jit(solution)/shard_map/add | solution.py:111
  17.4 1.3 collective-permute-start.3
  18.7 5.9 %collective-permute-start.2 = (f32[8,32,1,384]{3,1,2,0:T(8,128)S(1)}, f32[8,32,1,384]{3,1,2,0:T(8,128)S(1)}, u32[]{:S(2)}, u32[]{:S(2)}) collective-permute-start(f32[8,32,1,384]{3,1,2,0:T(8,128)S(1)} %get-tuple-element.58), channel_id=1, source_target_pairs={{0,8},{8,16},{16,24},{24,32},{32,40},{40,48},{48,56},{56,64},{64,7... | collective-permute-start | bytes 1179656 | tf_op jit(solution)/shard_map/ppermute | solution.py:51
  24.6 5.3 %collective-permute-done.3 = f32[8,32,1,384]{3,1,2,0:T(8,128)S(1)} collective-permute-done((f32[8,32,1,384]{3,1,2,0:T(8,128)S(1)}, f32[8,32,1,384]{3,1,2,0:T(8,128)S(1)}, u32[]{:S(2)}, u32[]{:S(2)}) %collective-permute-start.3) | collective-permute-done | bytes 393248 | tf_op jit(solution)/shard_map/ppermute | solution.py:53
  30.0 0.9 collective-permute-done.2
  30.9 3.7 %fusion.34 = f32[8,32,6,384]{3,1,2,0:T(8,128)S(1)} fusion(f32[8,32,6,384]{3,1,2,0:T(8,128)S(1)} %fusion.51, f32[8,32,1,384]{3,1,2,0:T(8,128)S(1)} %collective-permute-done.3, f32[8,32,1,384]{3,1,2,0:T(8,128)S(1)} %collective-permute-done.2, f32[32,6,384]{2,0,1:T(8,128)S(1)} %get-tuple-element.65, f32[32,6,384]{2,0,1:T(8,128)S(1)} %get-tuple-element.66, ...), kind=kLoop, calls=%fused_computation.53 | loop fusion | flops 20054016 | bytes 7274496 | tf_op jit(solution)/shard_map/add | solution.py:111
  34.7 1.3 collective-permute-start.5
  36.0 5.2 %collective-permute-start.4 = (f32[8,32,1,384]{3,1,2,0:T(8,128)S(1)}, f32[8,32,1,384]{3,1,2,0:T(8,128)S(1)}, u32[]{:S(2)}, u32[]{:S(2)}) collective-permute-start(f32[8,32,1,384]{3,1,2,0:T(8,128)S(1)} %get-tuple-element.56), channel_id=1, source_target_pairs={{0,8},{8,16},{16,24},{24,32},{32,40},{40,48},{48,56},{56,64},{64,7... | collective-permute-start | bytes 1179656 | tf_op jit(solution)/shard_map/ppermute | solution.py:51
  41.2 4.9 %collective-permute-done.5 = f32[8,32,1,384]{3,1,2,0:T(8,128)S(1)} collective-permute-done((f32[8,32,1,384]{3,1,2,0:T(8,128)S(1)}, f32[8,32,1,384]{3,1,2,0:T(8,128)S(1)}, u32[]{:S(2)}, u32[]{:S(2)}) %collective-permute-start.5) | collective-permute-done | bytes 393248 | tf_op jit(solution)/shard_map/ppermute | solution.py:53
  46.1 0.9 collective-permute-done.4
  47.1 3.7 %fusion.91 = f32[8,6,4,8,384]{4,3,2,1,0:T(8,128)S(1)} fusion(f32[8,32,6,384]{3,1,2,0:T(8,128)S(1)} %fusion.34, f32[32,6,384]{2,0,1:T(8,128)S(1)} %get-tuple-element.65, f32[32,6,384]{2,0,1:T(8,128)S(1)} %get-tuple-element.66, f32[32,6,384]{2,0,1:T(8,128)S(1)} %get-tuple-element.64, f32[32,6,384]{2,0,1:T(8,128)S(1)} %get-tuple-element.67, ...), kind=kLoop, calls=%fused_computation.147 | loop fusion | flops 20054016 | bytes 7274496
  51.0 1.4 copy-done
  52.4 5.2 %collective-permute-start.6 = (f32[8,32,2304]{2,1,0:T(8,128)S(1)}, f32[8,32,2304]{2,1,0:T(8,128)}, u32[]{:S(2)}, u32[]{:S(2)}) collective-permute-start(f32[8,32,2304]{2,1,0:T(8,128)S(1)} %bitcast.97), channel_id=1, source_target_pairs={{0,1},{1,2},{2,3},{3,4},{4,5},{5,6},{6,7},{7,0},{8,9},{9,10},{10,1... | collective-permute-start | bytes 7077896 | tf_op jit(solution)/shard_map/ppermute | solution.py:32
  57.6 25.8 %collective-permute-done.6 = f32[8,32,2304]{2,1,0:T(8,128)} collective-permute-done((f32[8,32,2304]{2,1,0:T(8,128)S(1)}, f32[8,32,2304]{2,1,0:T(8,128)}, u32[]{:S(2)}, u32[]{:S(2)}) %collective-permute-start.6) | collective-permute-done | bytes 2359328 | tf_op jit(solution)/shard_map/ppermute | solution.py:32
  83.4 2.6 %collective-permute-start.7 = (f32[8,32,2304]{2,1,0:T(8,128)}, f32[8,32,2304]{2,1,0:T(8,128)}, u32[]{:S(2)}, u32[]{:S(2)}) collective-permute-start(f32[8,32,2304]{2,1,0:T(8,128)} %collective-permute-done.6), channel_id=1, source_target_pairs={{0,1},{1,2},{2,3},{3,4},{4,5},{5,6},{6,7},{7,0},{8,9},{9,10},{10,1... | collective-permute-start | bytes 7077896 | tf_op jit(solution)/shard_map/ppermute | solution.py:32
  86.0 6.8 %copy.29 = f32[8,32,2304]{1,0,2:T(8,128)} copy(f32[8,32,2304]{2,1,0:T(8,128)} %bitcast.98) | data formatting | bytes 4718592 | tf_op jit(solution)/shard_map/reshape | solution.py:165
  92.8 4.3 %gather_fusion = f32[16,8,32]{2,1,0:T(8,128)S(1)} fusion(f32[8,32,2304]{1,0,2:T(8,128)} %copy.29, s32[1024]{0:T(1024)S(1)} %pad_clamp_fusion.1), kind=kCustom, calls=%fused_computation | custom fusion | bytes 32832 | tf_op jit(solution)/shard_map/jit(_take)/gather | solution.py:167
  97.3 0.9 reshape.128
  98.2 4.1 %all-to-all-start = ((f32[8,1,4096]{2,1,0:T(1,128)}), f32[8,1,4096]{2,1,0:T(1,128)S(1)}, u32[]{:S(2)}, u32[]{:S(2)}) async-start(f32[8,1,4096]{2,1,0:T(1,128)} %reshape.128), calls=%async_computation | async-start | bytes 262144 | tf_op jit(solution)/shard_map/all_to_all | solution.py:68
  102.3 0.7 reshape.102
  103.0 13.3 %all-to-all-done = f32[8,1,4096]{2,1,0:T(1,128)S(1)} async-done(((f32[8,1,4096]{2,1,0:T(1,128)}), f32[8,1,4096]{2,1,0:T(1,128)S(1)}, u32[]{:S(2)}, u32[]{:S(2)}) %all-to-all-start) | async-done | bytes 131104 | tf_op jit(solution)/shard_map/all_to_all | solution.py:68
  116.3 0.6 broadcast.186
  116.9 1.6 reduce.3
  118.4 1.1 reshape.129
  119.6 0.6 broadcast_multiply_fusion
  120.3 0.7 convolution_bitcast_fusion.1
  121.0 0.7 reshape.98
  121.8 1.4 convolution_bitcast_fusion.4
  123.1 0.7 pad_maximum_fusion.6
  123.9 1.1 broadcast_in_dim.26
  125.0 17.1 %all-to-all-start.1 = ((f32[32,1,4160]{2,1,0:T(1,128)}), f32[32,1,4160]{2,1,0:T(1,128)}, u32[]{:S(2)}, u32[]{:S(2)}) async-start(f32[32,1,4160]{2,1,0:T(1,128)} %broadcast_in_dim.26), calls=%async_computation.1 | async-start | bytes 1081344 | tf_op jit(solution)/shard_map/all_to_all | solution.py:68
  142.1 5.0 %fusion.17 = f32[8,32,6,384]{3,1,2,0:T(8,128)S(1)} fusion(f32[8,32,6,384]{3,1,2,0:T(8,128)S(1)} %fusion.34, f32[8,32,1,384]{3,1,2,0:T(8,128)} %copy-done.8, f32[8,32,1,384]{3,1,2,0:T(8,128)} %copy-done.9, f32[32,6,384]{2,0,1:T(8,128)} %copy-done.4, f32[32,6,384]{2,0,1:T(8,128)} %copy-done.5, f32[32,6,384]{2,0,1:T(8,128)S(1)} %copy-done.3, ...), kind=kLoop, calls=%fused_computation.34 | loop fusion | flops 20054016 | bytes 7274496 | tf_op jit(solution)/shard_map/add | solution.py:111
  147.1 1.4 copy.28
  148.5 1.7 stack_reshape.3
  150.2 6.5 %all-to-all-done.1 = f32[32,1,4160]{2,1,0:T(1,128)} async-done(((f32[32,1,4160]{2,1,0:T(1,128)}), f32[32,1,4160]{2,1,0:T(1,128)}, u32[]{:S(2)}, u32[]{:S(2)}) %all-to-all-start.1) | async-done | bytes 532512 | tf_op jit(solution)/shard_map/all_to_all | solution.py:68
  156.7 1.4 reduce_sum.28
  158.1 0.7 multiply_reduce_fusion
  159.7 2.9 %collective-permute-start.11 = (f32[8,32,2304]{2,1,0:T(8,128)}, f32[8,32,2304]{2,1,0:T(8,128)S(1)}, u32[]{:S(2)}, u32[]{:S(2)}) collective-permute-start(f32[8,32,2304]{2,1,0:T(8,128)} %collective-permute-done.10), channel_id=1, source_target_pairs={{1,0},{2,1},{3,2},{4,3},{5,4},{6,5},{7,6},{0,7},{9,8},{10,9},{11,1... | collective-permute-start | bytes 7077896 | tf_op jit(solution)/shard_map/ppermute | solution.py:35
  162.6 2.6 while.13
  162.8 0.2 convolution_bitcast_fusion.6
  163.5 0.2 convolution_bitcast_fusion.6
  164.1 0.2 convolution_bitcast_fusion.6
  165.5 0.3 fusion.64
  165.9 22.8 %collective-permute-done.11 = f32[8,32,2304]{2,1,0:T(8,128)S(1)} collective-permute-done((f32[8,32,2304]{2,1,0:T(8,128)}, f32[8,32,2304]{2,1,0:T(8,128)S(1)}, u32[]{:S(2)}, u32[]{:S(2)}) %collective-permute-start.11) | collective-permute-done | bytes 2359328 | tf_op jit(solution)/shard_map/ppermute | solution.py:35
  188.7 2.3 collective-permute-start.12
  191.0 3.3 %bitcast_dynamic-update-slice_fusion.6 = f32[8,8,32,2304]{3,2,1,0:T(8,128)} fusion(f32[8,32,2304]{2,1,0:T(8,128)} %collective-permute-done.9), kind=kLoop, calls=%fused_computation.85 | loop fusion | bytes 4718592
  194.3 3.3 %bitcast_dynamic-update-slice_fusion.5 = f32[8,8,32,2304]{3,2,1,0:T(8,128)} fusion(f32[8,8,32,2304]{3,2,1,0:T(8,128)} %bitcast_dynamic-update-slice_fusion.6, f32[8,32,2304]{2,1,0:T(8,128)} %collective-permute-done.8), kind=kLoop, calls=%fused_computation.84 | loop fusion | bytes 4718592
  197.6 3.3 %bitcast_dynamic-update-slice_fusion.4 = f32[8,8,32,2304]{3,2,1,0:T(8,128)} fusion(f32[8,8,32,2304]{3,2,1,0:T(8,128)} %bitcast_dynamic-update-slice_fusion.5, f32[8,32,2304]{2,1,0:T(8,128)} %collective-permute-done.7), kind=kLoop, calls=%fused_computation.83 | loop fusion | bytes 4718592
  200.9 3.5 %bitcast_dynamic-update-slice_fusion.3 = f32[8,8,32,2304]{3,2,1,0:T(8,128)} fusion(f32[8,8,32,2304]{3,2,1,0:T(8,128)} %bitcast_dynamic-update-slice_fusion.4, f32[8,32,2304]{2,1,0:T(8,128)} %collective-permute-done.6), kind=kLoop, calls=%fused_computation.82 | loop fusion | bytes 4718592
  204.4 1.6 constant_dynamic-update-slice_fusion
  205.9 3.3 %bitcast_dynamic-update-slice_fusion.2 = f32[8,8,32,2304]{3,2,1,0:T(8,128)} fusion(f32[8,8,32,2304]{3,2,1,0:T(8,128)} %constant_dynamic-update-slice_fusion, f32[8,32,2304]{2,1,0:T(8,128)} %collective-permute-done.10), kind=kLoop, calls=%fused_computation.81 | loop fusion | bytes 4718592
  209.2 1.6 bitcast_dynamic-update-slice_fusion.1
  210.8 6.1 %collective-permute-done.12 = f32[8,32,2304]{2,1,0:T(8,128)S(1)} collective-permute-done((f32[8,32,2304]{2,1,0:T(8,128)S(1)}, f32[8,32,2304]{2,1,0:T(8,128)S(1)}, u32[]{:S(2)}, u32[]{:S(2)}) %collective-permute-start.12) | collective-permute-done | bytes 2359328 | tf_op jit(solution)/shard_map/ppermute | solution.py:35
  216.9 1.6 bitcast_dynamic-update-slice_fusion
  218.5 15.3 %gather_fusion.1 = f32[8,8,32,2304]{3,2,1,0:T(8,128)} fusion(f32[8,8,32,2304]{3,2,1,0:T(8,128)} %bitcast_dynamic-update-slice_fusion, s32[1024]{0:T(1024)S(1)} %pad_clamp_fusion), kind=kCustom, calls=%fused_computation.1 | custom fusion | bytes 37748768 | tf_op jit(solution)/shard_map/gather | solution.py:39
  233.8 12.3 %copy.36 = f32[64,32,2304]{2,0,1:T(8,128)S(1)} copy(f32[64,32,2304]{2,1,0:T(8,128)} %bitcast.95) | data formatting | bytes 37748736 | tf_op jit(solution)/shard_map/reshape | solution.py:14
  246.2 9.1 %fusion.3 = f32[8,32,6,384]{3,0,2,1:T(8,128)S(1)} fusion(f32[32,8,6,8,384]{4,3,2,1,0:T(8,128)S(1)} %bitcast.96, f32[64,64]{0,1:T(8,128)S(1)} %fusion.64, s32[]{:T(128)S(6)} %select_n.38), kind=kOutput, calls=%fused_computation.7 | convolution fusion | flops 452985344 | bytes 21237764 | tf_op jit(solution)/shard_map/jk,jzc->kzc/dot_general | solution.py:174
  255.2 2.1 copy.38
  (70 shorter events, 2.9 us)
Async XLA Ops:
  0.0 13.6 %copy-start.7 = (f32[8,32,6,384]{3,1,2,0:T(8,128)S(1)}, f32[8,32,6,384]{3,1,2,0:T(8,128)}, u32[]{:S(2)}) copy-start(f32[8,32,6,384]{3,1,2,0:T(8,128)} %param.7) | copy-start | bytes 7077892
  1.3 11.4 %collective-permute-start.1 = (f32[8,32,1,384]{3,1,2,0:T(8,128)S(1)}, f32[8,32,1,384]{3,1,2,0:T(8,128)S(1)}, u32[]{:S(2)}, u32[]{:S(2)}) collective-permute-start(f32[8,32,1,384]{3,1,2,0:T(8,128)S(1)} %get-tuple-element.61), channel_id=1, source_target_pairs={{8,0},{16,8},{24,16},{32,24},{40,32},{48,40},{56,48},{64,56},{72,6... | collective-permute-start | bytes 1179656 | tf_op jit(solution)/shard_map/ppermute | solution.py:53
  2.6 11.0 %collective-permute-start = (f32[8,32,1,384]{3,1,2,0:T(8,128)S(1)}, f32[8,32,1,384]{3,1,2,0:T(8,128)S(1)}, u32[]{:S(2)}, u32[]{:S(2)}) collective-permute-start(f32[8,32,1,384]{3,1,2,0:T(8,128)S(1)} %get-tuple-element.60), channel_id=1, source_target_pairs={{0,8},{8,16},{16,24},{24,32},{32,40},{40,48},{48,56},{56,64},{64,7... | collective-permute-start | bytes 1179656 | tf_op jit(solution)/shard_map/ppermute | solution.py:51
  8.9 38.1 %copy-start.2 = (f32[32,6,384]{2,0,1:T(8,128)}, f32[32,6,384]{2,0,1:T(8,128)S(1)}, u32[]{:S(2)}) copy-start(f32[32,6,384]{2,0,1:T(8,128)S(1)} %get-tuple-element.64) | copy-start | bytes 884740
  8.9 38.1 %copy-start.4 = (f32[32,6,384]{2,0,1:T(8,128)}, f32[32,6,384]{2,0,1:T(8,128)S(1)}, u32[]{:S(2)}) copy-start(f32[32,6,384]{2,0,1:T(8,128)S(1)} %get-tuple-element.65) | copy-start | bytes 884740
  8.9 38.1 %copy-start.5 = (f32[32,6,384]{2,0,1:T(8,128)}, f32[32,6,384]{2,0,1:T(8,128)S(1)}, u32[]{:S(2)}) copy-start(f32[32,6,384]{2,0,1:T(8,128)S(1)} %get-tuple-element.66) | copy-start | bytes 884740
  9.0 38.1 %copy-start.6 = (f32[32,6,384]{2,0,1:T(8,128)}, f32[32,6,384]{2,0,1:T(8,128)S(1)}, u32[]{:S(2)}) copy-start(f32[32,6,384]{2,0,1:T(8,128)S(1)} %get-tuple-element.67) | copy-start | bytes 884740
  17.4 12.5 %collective-permute-start.3 = (f32[8,32,1,384]{3,1,2,0:T(8,128)S(1)}, f32[8,32,1,384]{3,1,2,0:T(8,128)S(1)}, u32[]{:S(2)}, u32[]{:S(2)}) collective-permute-start(f32[8,32,1,384]{3,1,2,0:T(8,128)S(1)} %get-tuple-element.59), channel_id=1, source_target_pairs={{8,0},{16,8},{24,16},{32,24},{40,32},{48,40},{56,48},{64,56},{72,6... | collective-permute-start | bytes 1179656 | tf_op jit(solution)/shard_map/ppermute | solution.py:53
  18.7 12.1 %collective-permute-start.2 = (f32[8,32,1,384]{3,1,2,0:T(8,128)S(1)}, f32[8,32,1,384]{3,1,2,0:T(8,128)S(1)}, u32[]{:S(2)}, u32[]{:S(2)}) collective-permute-start(f32[8,32,1,384]{3,1,2,0:T(8,128)S(1)} %get-tuple-element.58), channel_id=1, source_target_pairs={{0,8},{8,16},{16,24},{24,32},{32,40},{40,48},{48,56},{56,64},{64,7... | collective-permute-start | bytes 1179656 | tf_op jit(solution)/shard_map/ppermute | solution.py:51
  34.7 11.5 %collective-permute-start.5 = (f32[8,32,1,384]{3,1,2,0:T(8,128)S(1)}, f32[8,32,1,384]{3,1,2,0:T(8,128)S(1)}, u32[]{:S(2)}, u32[]{:S(2)}) collective-permute-start(f32[8,32,1,384]{3,1,2,0:T(8,128)S(1)} %get-tuple-element.57), channel_id=1, source_target_pairs={{8,0},{16,8},{24,16},{32,24},{40,32},{48,40},{56,48},{64,56},{72,6... | collective-permute-start | bytes 1179656 | tf_op jit(solution)/shard_map/ppermute | solution.py:53
  36.0 11.1 %collective-permute-start.4 = (f32[8,32,1,384]{3,1,2,0:T(8,128)S(1)}, f32[8,32,1,384]{3,1,2,0:T(8,128)S(1)}, u32[]{:S(2)}, u32[]{:S(2)}) collective-permute-start(f32[8,32,1,384]{3,1,2,0:T(8,128)S(1)} %get-tuple-element.56), channel_id=1, source_target_pairs={{0,8},{8,16},{16,24},{24,32},{32,40},{40,48},{48,56},{56,64},{64,7... | collective-permute-start | bytes 1179656 | tf_op jit(solution)/shard_map/ppermute | solution.py:51
  46.1 4.7 %copy-start.8 = (f32[8,32,1,384]{3,1,2,0:T(8,128)}, f32[8,32,1,384]{3,1,2,0:T(8,128)S(1)}, u32[]{:S(2)}) copy-start(f32[8,32,1,384]{3,1,2,0:T(8,128)S(1)} %collective-permute-done.5) | copy-start | bytes 1179652
  47.1 3.8 %copy-start.9 = (f32[8,32,1,384]{3,1,2,0:T(8,128)}, f32[8,32,1,384]{3,1,2,0:T(8,128)S(1)}, u32[]{:S(2)}) copy-start(f32[8,32,1,384]{3,1,2,0:T(8,128)S(1)} %collective-permute-done.4) | copy-start | bytes 1179652
  50.8 35.2 %copy-start.13 = (s32[16]{0:T(128)S(1)}, s32[16]{0:T(128)}, u32[]{:S(2)}) copy-start(s32[16]{0:T(128)} %param.9) | copy-start | bytes 196
  51.0 1.4 copy-start
  52.4 31.0 %collective-permute-start.6 = (f32[8,32,2304]{2,1,0:T(8,128)S(1)}, f32[8,32,2304]{2,1,0:T(8,128)}, u32[]{:S(2)}, u32[]{:S(2)}) collective-permute-start(f32[8,32,2304]{2,1,0:T(8,128)S(1)} %bitcast.97), channel_id=1, source_target_pairs={{0,1},{1,2},{2,3},{3,4},{4,5},{5,6},{6,7},{7,0},{8,9},{9,10},{10,1... | collective-permute-start | bytes 7077896 | tf_op jit(solution)/shard_map/ppermute | solution.py:32
  83.4 36.8 %collective-permute-start.7 = (f32[8,32,2304]{2,1,0:T(8,128)}, f32[8,32,2304]{2,1,0:T(8,128)}, u32[]{:S(2)}, u32[]{:S(2)}) collective-permute-start(f32[8,32,2304]{2,1,0:T(8,128)} %collective-permute-done.6), channel_id=1, source_target_pairs={{0,1},{1,2},{2,3},{3,4},{4,5},{5,6},{6,7},{7,0},{8,9},{9,10},{10,1... | collective-permute-start | bytes 7077896 | tf_op jit(solution)/shard_map/ppermute | solution.py:32
  92.8 26.8 %copy-start.11 = (f32[32,16]{0,1:T(8,128)S(1)}, f32[32,16]{0,1:T(8,128)}, u32[]{:S(2)}) copy-start(f32[32,16]{0,1:T(8,128)} %param.11) | copy-start | bytes 6148
  92.8 26.8 %copy-start.12 = (f32[32,16]{0,1:T(8,128)S(1)}, f32[32,16]{0,1:T(8,128)}, u32[]{:S(2)}) copy-start(f32[32,16]{0,1:T(8,128)} %param.10) | copy-start | bytes 6148
  98.2 18.1 %all-to-all-start = ((f32[8,1,4096]{2,1,0:T(1,128)}), f32[8,1,4096]{2,1,0:T(1,128)S(1)}, u32[]{:S(2)}, u32[]{:S(2)}) async-start(f32[8,1,4096]{2,1,0:T(1,128)} %reshape.128), calls=%async_computation | async-start | bytes 262144 | tf_op jit(solution)/shard_map/all_to_all | solution.py:68
  103.0 56.7 %collective-permute-start.10 = (f32[8,32,2304]{2,1,0:T(8,128)}, f32[8,32,2304]{2,1,0:T(8,128)}, u32[]{:S(2)}, u32[]{:S(2)}) collective-permute-start(f32[8,32,2304]{2,1,0:T(8,128)} %bitcast.99), channel_id=1, source_target_pairs={{1,0},{2,1},{3,2},{4,3},{5,4},{6,5},{7,6},{0,7},{9,8},{10,9},{11,1... | collective-permute-start | bytes 7077896 | tf_op jit(solution)/shard_map/ppermute | solution.py:35
  120.2 42.4 %collective-permute-start.8 = (f32[8,32,2304]{2,1,0:T(8,128)}, f32[8,32,2304]{2,1,0:T(8,128)}, u32[]{:S(2)}, u32[]{:S(2)}) collective-permute-start(f32[8,32,2304]{2,1,0:T(8,128)} %collective-permute-done.7), channel_id=1, source_target_pairs={{0,1},{1,2},{2,3},{3,4},{4,5},{5,6},{6,7},{7,0},{8,9},{9,10},{10,1... | collective-permute-start | bytes 7077896 | tf_op jit(solution)/shard_map/ppermute | solution.py:32
  121.7 20.3 %copy-start.3 = (f32[32,6,384]{2,0,1:T(8,128)S(1)}, f32[32,6,384]{2,0,1:T(8,128)}, u32[]{:S(2)}) copy-start(f32[32,6,384]{2,0,1:T(8,128)} %copy-done.2) | copy-start | bytes 884740
  125.0 31.8 %all-to-all-start.1 = ((f32[32,1,4160]{2,1,0:T(1,128)}), f32[32,1,4160]{2,1,0:T(1,128)}, u32[]{:S(2)}, u32[]{:S(2)}) async-start(f32[32,1,4160]{2,1,0:T(1,128)} %broadcast_in_dim.26), calls=%async_computation.1 | async-start | bytes 1081344 | tf_op jit(solution)/shard_map/all_to_all | solution.py:68
  148.5 9.6 %copy-start.10 = (f32[4096]{0:T(1024)S(1)}, f32[4096]{0:T(1024)}, u32[]{:S(2)}) copy-start(f32[4096]{0:T(1024)} %reshape.102) | copy-start | bytes 49156
  159.7 29.0 %collective-permute-start.11 = (f32[8,32,2304]{2,1,0:T(8,128)}, f32[8,32,2304]{2,1,0:T(8,128)S(1)}, u32[]{:S(2)}, u32[]{:S(2)}) collective-permute-start(f32[8,32,2304]{2,1,0:T(8,128)} %collective-permute-done.10), channel_id=1, source_target_pairs={{1,0},{2,1},{3,2},{4,3},{5,4},{6,5},{7,6},{0,7},{9,8},{10,9},{11,1... | collective-permute-start | bytes 7077896 | tf_op jit(solution)/shard_map/ppermute | solution.py:35
  162.6 28.4 %collective-permute-start.9 = (f32[8,32,2304]{2,1,0:T(8,128)}, f32[8,32,2304]{2,1,0:T(8,128)}, u32[]{:S(2)}, u32[]{:S(2)}) collective-permute-start(f32[8,32,2304]{2,1,0:T(8,128)} %collective-permute-done.8), channel_id=1, source_target_pairs={{0,1},{1,2},{2,3},{3,4},{4,5},{5,6},{6,7},{7,0},{8,9},{9,10},{10,1... | collective-permute-start | bytes 7077896 | tf_op jit(solution)/shard_map/ppermute | solution.py:32
  188.7 28.3 %collective-permute-start.12 = (f32[8,32,2304]{2,1,0:T(8,128)S(1)}, f32[8,32,2304]{2,1,0:T(8,128)S(1)}, u32[]{:S(2)}, u32[]{:S(2)}) collective-permute-start(f32[8,32,2304]{2,1,0:T(8,128)S(1)} %collective-permute-done.11), channel_id=1, source_target_pairs={{1,0},{2,1},{3,2},{4,3},{5,4},{6,5},{7,6},{0,7},{9,8},{10,9},{11,1... | collective-permute-start | bytes 7077896 | tf_op jit(solution)/shard_map/ppermute | solution.py:35
  200.9 3.5 %copy-start.1 = (f32[1,8,32,2304]{3,2,1,0:T(8,128)S(1)}, f32[1,8,32,2304]{3,2,1,0:T(8,128)}, u32[]{:S(2)}) copy-start(f32[1,8,32,2304]{3,2,1,0:T(8,128)} %stack_reshape.3) | copy-start | bytes 7077892
